TPU v7x, 32 devices: a whole 2x2x4 slice. The times are simulated.
32 devices in a mesh: body: 16 (over z, x, core), row: 2 (over y).
Axes of the slice: x: 2, y: 2, z: 4, core: 2. Of those that a mesh axis runs over, the one named last changes fastest.
Arguments:
- strengths: bfloat16 [32, 131072], P(None, ('body', 'row')), may hold values from -6 to 6
- influence: bfloat16 [16, 2, 5, 32, 2, 128, 128], P('body', 'row'), may hold values from -0.09375 to 0.09375
- target_block: int32 [16, 2, 5, 32], P('body', 'row'), may hold values from 0 to 31
- source_block: int32 [16, 2, 5, 32], P('body', 'row'), may hold values from 0 to 63
- live_counts: int32 [16, 2, 5], P('body', 'row'), may hold values from 4 to 32, as said below
Outputs:
- response: float32 [32, 131072], P(None, ('body', 'row'))
Inputs may be any that keep to these rules, and one draw needn't show every extreme that they name: Slot k of a slice for source offset t is live when k < live_counts; for offset 2 (the group's own bodies) all 32 slots are live.
All inputs are finite; a program needn't handle non-finite values.
Results may differ from a plain program's by a relative error of at most 0.0003.
Values may be sent and summed in bfloat16 or wider, within the bound.
No kernel may reach another device: no remote copies, remote signals or barrier semaphores. Data moves between devices by JAX's collectives and lax.ppermute only.
A program may use at most 64 MiB of HBM per device.

v0:
```python
import jax
import jax.numpy as jnp
from jax import lax
from jax.sharding import PartitionSpec as P


def passed_along(array, axis, by):
    devices = lax.axis_size(axis)
    return lax.ppermute(array, axis, [(i, (i + by) % devices) for i in range(devices)])


def block_terms(slot_tiles, slot_rows, live_count, picked, row_blocks):
    channels = picked.shape[0]
    heads = channels // 2
    capacity = slot_tiles.shape[0]
    products = jnp.einsum("kprj,hkj->kphr", slot_tiles, picked, preferred_element_type=jnp.float32)
    real_part = products[:, 0, :heads] - products[:, 1, heads:]
    imag_part = products[:, 0, heads:] + products[:, 1, :heads]
    combined = jnp.concatenate([real_part, imag_part], axis=1)
    alive_mask = (jnp.arange(capacity, dtype=jnp.int32) < live_count).astype(jnp.float32)
    onehot = (slot_rows[:, None] == jnp.arange(row_blocks, dtype=jnp.int32)[None, :]).astype(
        jnp.float32
    )
    onehot = onehot * alive_mask[:, None]
    return jnp.einsum("kn,khr->hnr", onehot, combined, precision=lax.Precision.HIGHEST)


def pick_blocks(group_x, slot_cols, block_size):
    channels = group_x.shape[0]
    blocks = group_x.reshape(channels, -1, block_size)
    return jnp.take(blocks, slot_cols, axis=1)


def window(values, reach):
    windows = [(0, values)]
    for direction in (1, -1):
        current = values
        for hop_index in range(reach):
            current = passed_along(current, "body", direction)
            windows.append((-direction * (hop_index + 1), current))
    return windows


def on_device(strengths, influence, target_block, source_block, live_counts):
    channels, row_count = strengths.shape
    block_size = influence.shape[-1]
    row_blocks = row_count // block_size
    reach = (influence.shape[2] - 1) // 2
    totals = (0.5 * strengths.astype(jnp.float32)).reshape(channels, row_blocks, block_size)

    def apply_picked(totals_now, offset, picked):
        index = offset + reach
        return totals_now + block_terms(
            influence[0, 0, index],
            target_block[0, 0, index],
            live_counts[0, 0, index],
            picked,
            row_blocks,
        )

    def apply_offset(totals_now, offset, group_x):
        index = offset + reach
        picked = pick_blocks(group_x, source_block[0, 0, index], block_size)
        return apply_picked(totals_now, offset, picked)

    group_x = lax.all_gather(strengths, "row", axis=1, tiled=True)
    for offset, source_x in window(group_x, reach):
        totals = apply_offset(totals, offset, source_x)
    return totals.reshape(channels, row_count)


def solution(mesh):
    return jax.shard_map(
        on_device,
        mesh=mesh,
        in_specs=(
            P(None, ("body", "row")),
            P("body", "row", None, None, None, None, None),
            P("body", "row", None, None),
            P("body", "row", None, None),
            P("body", "row", None),
        ),
        out_specs=P(None, ("body", "row")),
        check_vma=False,
    )
```

profile of v0, /device:TPU:1, one launch (start us, length us, event | category | flops | bytes accessed | tf_op | source)
XLA Modules:
  0.0 56.6 jit_solution(6832906776811036869)
XLA Ops:
  0.0 9.0 %all_gather.3 = bf16[32,8192]{1,0:T(8,128)(2,1)S(1)} all-gather(bf16[32,4096]{1,0:T(8,128)(2,1)} %param.7), channel_id=1, replica_groups=mesh['body'=16,'row'=2] {'row'}, dimensions={1}, use_global_device_ids=true | all-gather | bytes 786432 | tf_op jit(solution)/shard_map/all_gather | solution.py:66
  9.0 2.5 %collective-permute-start = (bf16[32,8192]{1,0:T(8,128)(2,1)S(1)}, bf16[32,8192]{1,0:T(8,128)(2,1)S(1)}, u32[]{:S(2)}, u32[]{:S(2)}) collective-permute-start(bf16[32,8192]{1,0:T(8,128)(2,1)S(1)} %all_gather.3), channel_id=1, source_target_pairs={{0,2},{2,4},{4,6},{6,8},{8,10},{10,12},{12,14},{14,16},{16,18},{18... | collective-permute-start | bytes 1572872 | tf_op jit(solution)/shard_map/ppermute | solution.py:9
  11.5 0.0 collective-permute-start.2
  11.5 0.1 copy_bitcast_fusion.5
  11.6 1.0 %multiply_bitcast_fusion = f32[4,8,32,128]{3,1,2,0:T(8,128)S(1)} fusion(bf16[32,4096]{1,0:T(8,128)(2,1)} %param.7), kind=kLoop, calls=%fused_computation.51 | loop fusion | flops 262144 | bytes 786432
  12.6 0.7 %compare_and_fusion = (pred[32]{0:T(512)(128)(4,1)S(1)}, s32[32]{0:T(128)S(1)}, pred[32]{0:T(512)(128)(4,1)S(1)}, s32[32]{0:T(128)S(1)}, pred[32]{0:T(512)(128)(...) fusion(s32[1,1,5,32]{3,1,2,0:T(1,128)} %param.10), kind=kLoop, calls=%fused_computation.142 | loop fusion | flops 960 | bytes 1440 | tf_op jit(solution)/shard_map/jit(_take)/and | solution.py:31
  13.4 1.5 %fusion.110 = (s32[1,1,1]{2,1,0:T(1,128)}, s32[1,1,1]{2,1,0:T(1,128)}, s32[1,1,1]{2,1,0:T(1,128)}, s32[1,1,1]{2,1,0:T(1,128)}, s32[1,1,1]{2,1,0:T(1,128)}) fusion(s32[1,1,5]{2,1,0:T(1,128)} %param.11), kind=kLoop, calls=%fused_computation.167 | loop fusion | bytes 40 | tf_op jit(solution)/shard_map/slice | solution.py:56
  14.8 0.6 %compare_convert_fusion.2 = f32[32]{0:T(128)S(1)} fusion(s32[]{:T(128)} %bitcast.33), kind=kLoop, calls=%fused_computation.149 | loop fusion | flops 64 | bytes 132 | tf_op jit(solution)/shard_map/convert_element_type | solution.py:20
  15.4 0.6 %compare_convert_fusion.3 = f32[32]{0:T(128)S(1)} fusion(s32[]{:T(128)} %bitcast.21), kind=kLoop, calls=%fused_computation.150 | loop fusion | flops 64 | bytes 132 | tf_op jit(solution)/shard_map/convert_element_type | solution.py:20
  16.1 0.6 %compare_convert_fusion.1 = f32[32]{0:T(128)S(1)} fusion(s32[]{:T(128)} %bitcast.45), kind=kLoop, calls=%fused_computation.148 | loop fusion | flops 64 | bytes 132 | tf_op jit(solution)/shard_map/convert_element_type | solution.py:20
  16.7 0.6 %gather_fusion = bf16[32,32,128]{2,1,0:T(8,128)(2,1)S(1)} fusion(bf16[32,64,128]{2,0,1:T(8,128)(2,1)S(1)} %copy_bitcast_fusion.5, s32[1024]{0:T(1024)S(1)} %pad_clamp_fusion.4), kind=kCustom, calls=%fused_computation.clone | custom fusion | bytes 524416 | tf_op jit(solution)/shard_map/jit(_take)/gather | solution.py:31
  17.3 2.4 %fusion.15 = f32[32,2,32,128]{3,2,1,0:T(8,128)S(1)} fusion(bf16[1,1,5,32,2,128,128]{6,5,4,3,2,1,0:T(8,128)(2,1)} %param.8, bf16[32,32,128]{2,1,0:T(8,128)(2,1)S(1)} %gather_fusion, pred[32]{0:T(512)(128)(4,1)S(1)} %get-tuple-element.25), kind=kOutput, calls=%fused_computation.20 | convolution fusion | flops 67239936 | bytes 3407904 | tf_op jit(solution)/shard_map/kprj,hkj->kphr/dot_general | solution.py:16
  19.8 0.6 %compare_convert_fusion.4 = f32[32]{0:T(128)S(1)} fusion(s32[]{:T(128)} %bitcast.9), kind=kLoop, calls=%fused_computation.151 | loop fusion | flops 64 | bytes 132 | tf_op jit(solution)/shard_map/convert_element_type | solution.py:20
  20.4 0.1 copy.76
  20.6 0.7 %compare_convert_fusion = f32[32]{0:T(128)S(1)} fusion(s32[]{:T(128)} %bitcast.57), kind=kLoop, calls=%fused_computation.147 | loop fusion | flops 64 | bytes 132 | tf_op jit(solution)/shard_map/convert_element_type | solution.py:20
  21.3 0.1 pad_maximum_fusion
  21.3 0.7 %slice_bitcast_fusion.10 = (s32[32]{0:T(128)S(1)}, s32[32]{0:T(128)S(1)}, s32[32]{0:T(128)S(1)}, s32[32]{0:T(128)S(1)}, s32[32]{0:T(128)S(1)}) fusion(s32[1,1,5,32]{3,1,2,0:T(1,128)} %param.9), kind=kLoop, calls=%fused_computation.152 | loop fusion | bytes 1280 | tf_op jit(solution)/shard_map/eq | solution.py:21
  22.1 1.2 %collective-permute-done = bf16[32,8192]{1,0:T(8,128)(2,1)S(1)} collective-permute-done((bf16[32,8192]{1,0:T(8,128)(2,1)S(1)}, bf16[32,8192]{1,0:T(8,128)(2,1)S(1)}, u32[]{:S(2)}, u32[]{:S(2)}) %collective-permute-start) | collective-permute-done | bytes 524320 | tf_op jit(solution)/shard_map/ppermute | solution.py:9
  23.3 0.1 copy_bitcast_fusion.4
  23.4 0.6 %gather_fusion.1 = bf16[32,32,128]{2,1,0:T(8,128)(2,1)S(1)} fusion(bf16[32,64,128]{2,0,1:T(8,128)(2,1)S(1)} %copy_bitcast_fusion.4, s32[1024]{0:T(1024)S(1)} %pad_clamp_fusion.3), kind=kCustom, calls=%fused_computation.1.clone | custom fusion | bytes 524416 | tf_op jit(solution)/shard_map/jit(_take)/gather | solution.py:31
  24.0 2.4 %fusion.18 = f32[32,2,32,128]{3,2,1,0:T(8,128)S(1)} fusion(bf16[1,1,5,32,2,128,128]{6,5,4,3,2,1,0:T(8,128)(2,1)} %param.8, bf16[32,32,128]{2,1,0:T(8,128)(2,1)S(1)} %gather_fusion.1, pred[32]{0:T(512)(128)(4,1)S(1)} %get-tuple-element.23), kind=kOutput, calls=%fused_computation.21 | convolution fusion | flops 67239936 | bytes 3407904 | tf_op jit(solution)/shard_map/kprj,hkj->kphr/dot_general | solution.py:16
  26.5 0.0 collective-permute-done.2
  26.5 1.1 %copy_bitcast_fusion.2 = bf16[32,64,128]{2,0,1:T(8,128)(2,1)S(1)} fusion(bf16[32,8192]{1,0:T(8,128)(2,1)} %collective-permute-done.2), kind=kLoop, calls=%fused_computation.37 | loop fusion | bytes 1048576 | tf_op jit(solution)/shard_map/reshape | solution.py:30
  27.6 0.6 %gather_fusion.3 = bf16[32,32,128]{2,1,0:T(8,128)(2,1)S(1)} fusion(bf16[32,64,128]{2,0,1:T(8,128)(2,1)S(1)} %copy_bitcast_fusion.2, s32[1024]{0:T(1024)S(1)} %pad_clamp_fusion.1), kind=kCustom, calls=%fused_computation.3.clone | custom fusion | bytes 524416 | tf_op jit(solution)/shard_map/jit(_take)/gather | solution.py:31
  28.2 2.4 %fusion.24 = f32[32,2,32,128]{3,2,1,0:T(8,128)S(1)} fusion(bf16[1,1,5,32,2,128,128]{6,5,4,3,2,1,0:T(8,128)(2,1)} %param.8, bf16[32,32,128]{2,1,0:T(8,128)(2,1)S(1)} %gather_fusion.3, pred[32]{0:T(512)(128)(4,1)S(1)} %get-tuple-element.27), kind=kOutput, calls=%fused_computation.23 | convolution fusion | flops 67239936 | bytes 3407904 | tf_op jit(solution)/shard_map/kprj,hkj->kphr/dot_general | solution.py:16
  30.8 0.1 pad_maximum_fusion.1
  30.8 2.5 %collective-permute-start.1 = (bf16[32,8192]{1,0:T(8,128)(2,1)S(1)}, bf16[32,8192]{1,0:T(8,128)(2,1)S(1)}, u32[]{:S(2)}, u32[]{:S(2)}) collective-permute-start(bf16[32,8192]{1,0:T(8,128)(2,1)S(1)} %collective-permute-done), channel_id=1, source_target_pairs={{0,2},{2,4},{4,6},{6,8},{8,10},{10,12},{12,14},{14,16},{16,18},{18... | collective-permute-start | bytes 1572872 | tf_op jit(solution)/shard_map/ppermute | solution.py:9
  33.3 0.1 pad_maximum_fusion.3
  33.4 0.1 collective-permute-start.3
  33.5 0.9 %convolution_bitcast_fusion.3 = f32[32,32,128]{2,1,0:T(8,128)S(1)} fusion(f32[32,32,128]{2,1,0:T(8,128)S(1)} %pad_maximum_fusion.1, f32[32]{0:T(128)S(1)} %compare_convert_fusion.3, s32[32]{0:T(128)S(1)} %get-tuple-element.18), kind=kOutput, calls=%fused_computation.28 | convolution fusion | flops 50333696 | bytes 1048832 | tf_op jit(solution)/shard_map/kn,khr->hnr/dot_general | solution.py:25
  34.4 0.9 %convolution_bitcast_fusion.1 = f32[32,32,128]{2,1,0:T(8,128)S(1)} fusion(f32[32,32,128]{2,1,0:T(8,128)S(1)} %pad_maximum_fusion.3, f32[32]{0:T(128)S(1)} %compare_convert_fusion.1, s32[32]{0:T(128)S(1)} %get-tuple-element.20), kind=kOutput, calls=%fused_computation.26 | convolution fusion | flops 50333696 | bytes 1048832 | tf_op jit(solution)/shard_map/kn,khr->hnr/dot_general | solution.py:25
  35.3 9.8 %collective-permute-done.1 = bf16[32,8192]{1,0:T(8,128)(2,1)S(1)} collective-permute-done((bf16[32,8192]{1,0:T(8,128)(2,1)S(1)}, bf16[32,8192]{1,0:T(8,128)(2,1)S(1)}, u32[]{:S(2)}, u32[]{:S(2)}) %collective-permute-start.1) | collective-permute-done | bytes 524320 | tf_op jit(solution)/shard_map/ppermute | solution.py:9
  45.1 0.1 copy_bitcast_fusion.3
  45.2 0.6 %gather_fusion.2 = bf16[32,32,128]{2,1,0:T(8,128)(2,1)S(1)} fusion(bf16[32,64,128]{2,0,1:T(8,128)(2,1)S(1)} %copy_bitcast_fusion.3, s32[1024]{0:T(1024)S(1)} %pad_clamp_fusion.2), kind=kCustom, calls=%fused_computation.2.clone | custom fusion | bytes 524416 | tf_op jit(solution)/shard_map/jit(_take)/gather | solution.py:31
  45.8 2.4 %fusion.21 = f32[32,2,32,128]{3,2,1,0:T(8,128)S(1)} fusion(bf16[1,1,5,32,2,128,128]{6,5,4,3,2,1,0:T(8,128)(2,1)} %param.8, bf16[32,32,128]{2,1,0:T(8,128)(2,1)S(1)} %gather_fusion.2, pred[32]{0:T(512)(128)(4,1)S(1)} %get-tuple-element.21), kind=kOutput, calls=%fused_computation.22 | convolution fusion | flops 67239936 | bytes 3407904 | tf_op jit(solution)/shard_map/kprj,hkj->kphr/dot_general | solution.py:16
  48.3 0.0 collective-permute-done.3
  48.3 1.1 %copy_bitcast_fusion.1 = bf16[32,64,128]{2,0,1:T(8,128)(2,1)S(1)} fusion(bf16[32,8192]{1,0:T(8,128)(2,1)} %collective-permute-done.3), kind=kLoop, calls=%fused_computation.36 | loop fusion | bytes 1048576 | tf_op jit(solution)/shard_map/reshape | solution.py:30
  49.5 0.6 %gather_fusion.4 = bf16[32,32,128]{2,1,0:T(8,128)(2,1)S(1)} fusion(bf16[32,64,128]{2,0,1:T(8,128)(2,1)S(1)} %copy_bitcast_fusion.1, s32[1024]{0:T(1024)S(1)} %pad_clamp_fusion), kind=kCustom, calls=%fused_computation.4.clone | custom fusion | bytes 524416 | tf_op jit(solution)/shard_map/jit(_take)/gather | solution.py:31
  50.1 2.4 %fusion.27 = f32[32,2,32,128]{3,2,1,0:T(8,128)S(1)} fusion(bf16[1,1,5,32,2,128,128]{6,5,4,3,2,1,0:T(8,128)(2,1)} %param.8, bf16[32,32,128]{2,1,0:T(8,128)(2,1)S(1)} %gather_fusion.4, pred[32]{0:T(512)(128)(4,1)S(1)} %get-tuple-element.6), kind=kOutput, calls=%fused_computation.24 | convolution fusion | flops 67239936 | bytes 3407904 | tf_op jit(solution)/shard_map/kprj,hkj->kphr/dot_general | solution.py:16
  52.6 0.1 pad_maximum_fusion.2
  52.6 0.1 pad_maximum_fusion.4
  52.7 0.9 %convolution_bitcast_fusion.2 = f32[32,32,128]{2,1,0:T(8,128)S(1)} fusion(f32[32,32,128]{2,1,0:T(8,128)S(1)} %pad_maximum_fusion.2, f32[32]{0:T(128)S(1)} %compare_convert_fusion.2, s32[32]{0:T(128)S(1)} %get-tuple-element.17), kind=kOutput, calls=%fused_computation.27 | convolution fusion | flops 50333696 | bytes 1048832 | tf_op jit(solution)/shard_map/kn,khr->hnr/dot_general | solution.py:25
  53.6 1.0 %fusion.33 = f32[32,32,128]{2,1,0:T(8,128)S(1)} fusion(f32[32,32,128]{2,1,0:T(8,128)S(1)} %convolution_bitcast_fusion.1, f32[32,32,128]{2,1,0:T(8,128)S(1)} %convolution_bitcast_fusion.2, f32[32,32,128]{2,1,0:T(8,128)S(1)} %convolution_bitcast_fusion.3, f32[32,32,128]{2,1,0:T(8,128)S(1)} %bitcast.237, f32[32,32,128]{2,1,0:T(8,128)S(1)} %pad_maximum_fusion, ...), kind=kOutput, calls=%fused_computation.33 | convolution fusion | flops 50857984 | bytes 3145984 | tf_op jit(solution)/shard_map/kn,khr->hnr/dot_general | solution.py:25
  54.6 0.9 %fusion.34 = f32[32,32,128]{2,1,0:T(8,128)S(1)} fusion(f32[32,32,128]{2,1,0:T(8,128)S(1)} %fusion.33, f32[32,32,128]{2,1,0:T(8,128)S(1)} %pad_maximum_fusion.4, f32[32]{0:T(128)S(1)} %compare_convert_fusion, s32[32]{0:T(128)S(1)} %get-tuple-element.16), kind=kOutput, calls=%fused_computation.34 | convolution fusion | flops 50464768 | bytes 1573120 | tf_op jit(solution)/shard_map/kn,khr->hnr/dot_general | solution.py:25
  55.5 1.1 %copy.94 = f32[4,8,32,128]{3,1,2,0:T(8,128)} copy(f32[4,8,32,128]{3,2,1,0:T(8,128)S(1)} %bitcast.238) | data formatting | bytes 1048576
  (15 shorter events, 0.4 us)
Async XLA Ops:
  9.0 14.2 %collective-permute-start = (bf16[32,8192]{1,0:T(8,128)(2,1)S(1)}, bf16[32,8192]{1,0:T(8,128)(2,1)S(1)}, u32[]{:S(2)}, u32[]{:S(2)}) collective-permute-start(bf16[32,8192]{1,0:T(8,128)(2,1)S(1)} %all_gather.3), channel_id=1, source_target_pairs={{0,2},{2,4},{4,6},{6,8},{8,10},{10,12},{12,14},{14,16},{16,18},{18... | collective-permute-start | bytes 1572872 | tf_op jit(solution)/shard_map/ppermute | solution.py:9
  11.5 15.0 %collective-permute-start.2 = (bf16[32,8192]{1,0:T(8,128)(2,1)S(1)}, bf16[32,8192]{1,0:T(8,128)(2,1)}, u32[]{:S(2)}, u32[]{:S(2)}) collective-permute-start(bf16[32,8192]{1,0:T(8,128)(2,1)S(1)} %all_gather.3), channel_id=1, source_target_pairs={{0,30},{2,0},{4,2},{6,4},{8,6},{10,8},{12,10},{14,12},{16,14},{18,... | collective-permute-start | bytes 1572872 | tf_op jit(solution)/shard_map/ppermute | solution.py:9
  30.8 14.3 %collective-permute-start.1 = (bf16[32,8192]{1,0:T(8,128)(2,1)S(1)}, bf16[32,8192]{1,0:T(8,128)(2,1)S(1)}, u32[]{:S(2)}, u32[]{:S(2)}) collective-permute-start(bf16[32,8192]{1,0:T(8,128)(2,1)S(1)} %collective-permute-done), channel_id=1, source_target_pairs={{0,2},{2,4},{4,6},{6,8},{8,10},{10,12},{12,14},{14,16},{16,18},{18... | collective-permute-start | bytes 1572872 | tf_op jit(solution)/shard_map/ppermute | solution.py:9
  33.4 14.9 %collective-permute-start.3 = (bf16[32,8192]{1,0:T(8,128)(2,1)}, bf16[32,8192]{1,0:T(8,128)(2,1)}, u32[]{:S(2)}, u32[]{:S(2)}) collective-permute-start(bf16[32,8192]{1,0:T(8,128)(2,1)} %collective-permute-done.2), channel_id=1, source_target_pairs={{0,30},{2,0},{4,2},{6,4},{8,6},{10,8},{12,10},{14,12},{16,14},{18,... | collective-permute-start | bytes 1572872 | tf_op jit(solution)/shard_map/ppermute | solution.py:9
where the time goes:
time: 57.1 us; the launch traced here: 56.6 us
  matrix products  16.8 us (29%)
  waiting for transfers between devices  11 us (19%)
  blocking collectives  9.02 us (16%)
  local copies, waits for them, and re-layouts  8.95 us (16%)
  other arithmetic  5.46 us (10%)
  starting transfers between devices  5.1 us (9%)
    dot_general x5, matrix products, block_terms(): jnp.einsum('kprj,hkj->kphr', slot_tiles, picked, preferred_element_type=j...  12.2 us
    ppermute x4, waiting for transfers between devices, passed_along(): lax.ppermute(array, axis, [(i, (i + by) % devices) for i in range(devices)])  11 us
    all_gather x1, blocking collectives, on_device(): group_x = lax.all_gather(strengths, 'row', axis=1, tiled=True)  9.02 us
    ppermute x4, starting transfers between devices, passed_along(): lax.ppermute(array, axis, [(i, (i + by) % devices) for i in range(devices)])  5.1 us
    dot_general x5, matrix products, block_terms(): jnp.einsum('kn,khr->hnr', onehot, combined, precision=lax.Precision.HIGHEST)  4.6 us
    convert_element_type x5, other arithmetic, block_terms(): (jnp.arange(capacity, dtype=jnp.int32) < live_count).astype(jnp.float32)  3.1 us
    gather x5, local copies, waits for them, and re-layouts, pick_blocks(): return jnp.take(blocks, slot_cols, axis=1)  3.01 us
    reshape x5, local copies, waits for them, and re-layouts, pick_blocks(): blocks = group_x.reshape(channels, -1, block_size)  2.54 us
  transfers between devices with their start and end apart: 4, of which 2 were waited for; matrix products, arithmetic and copies ran while one was open for 33% of the time, Pallas kernels for 0%

commit v1 on v0

--- a/solution.py
+++ b/solution.py
@@ -2,6 +2,19 @@
 import jax.numpy as jnp
 from jax import lax
 from jax.sharding import PartitionSpec as P
+
+
+def hold_the_field(s0):
+    mesh_ax = "row"
+    row_out, outer, clean = (lax.axis_size(mesh_ax), lax.axis_index(mesh_ax), s0.shape[1])
+    e_next, main = (s0, 1)
+    while main < row_out:
+        rows = []
+        for kk in range(row_out):
+            rows.append((kk, (kk - main) % row_out))
+        e_next = jnp.concatenate([e_next, lax.ppermute(e_next, mesh_ax, rows)], axis=1)
+        main = 2 * main
+    return jnp.roll(e_next, shift=outer * clean, axis=1)
 
 
 def passed_along(array, axis, by):
@@ -63,7 +76,7 @@
         picked = pick_blocks(group_x, source_block[0, 0, index], block_size)
         return apply_picked(totals_now, offset, picked)
 
-    group_x = lax.all_gather(strengths, "row", axis=1, tiled=True)
+    group_x = hold_the_field(strengths)
     for offset, source_x in window(group_x, reach):
         totals = apply_offset(totals, offset, source_x)
     return totals.reshape(channels, row_count)

time: 57.1 us -> 58.5 us (1.025)
  blocking collectives: 9.02 us -> 0 us
  waiting for transfers between devices: 11 us -> 17.7 us
  starting transfers between devices: 5.1 us -> 6.82 us
  other arithmetic: 5.46 us -> 7.06 us
    all_gather x1 -> x0, blocking collectives: 9.02 us -> none  [on_device(): group_x = lax.all_gather(strengths, 'row', axis=1, tiled=True)]
    ppermute x4, waiting for transfers between devices: 11 us -> 17.7 us  [passed_along(): lax.ppermute(array, axis, [(i, (i + by) % devices) for i in range(devices)])]
    ppermute x0 -> x1, starting transfers between devices: none -> 2.07 us  [hold_the_field(): lax.ppermute(e_next, mesh_ax, rows)]
    concatenate x0 -> x1, other arithmetic: none -> 1.51 us  [hold_the_field(): return jnp.roll(e_next, shift=outer * clean, axis=1)]
  transfers between devices with their start and end apart: 4 -> 5, of which waited for: 2 -> 2; matrix products, arithmetic and copies ran while one was open for 33% -> 33% of each run, Pallas kernels for 0% -> 0%
where the time goes in v1:
time: 58.5 us; the launch traced here: 57.7 us
  waiting for transfers between devices  17.7 us (30%)
  matrix products  16.8 us (29%)
  local copies, waits for them, and re-layouts  8.97 us (15%)
  other arithmetic  7.06 us (12%)
  starting transfers between devices  6.82 us (12%)
    ppermute x4, waiting for transfers between devices, passed_along(): lax.ppermute(array, axis, [(i, (i + by) % devices) for i in range(devices)])  17.7 us
    dot_general x5, matrix products, block_terms(): jnp.einsum('kprj,hkj->kphr', slot_tiles, picked, preferred_element_type=j...  12.2 us
    ppermute x4, starting transfers between devices, passed_along(): lax.ppermute(array, axis, [(i, (i + by) % devices) for i in range(devices)])  4.75 us
    dot_general x5, matrix products, block_terms(): jnp.einsum('kn,khr->hnr', onehot, combined, precision=lax.Precision.HIGHEST)  4.61 us
    convert_element_type x5, other arithmetic, block_terms(): (jnp.arange(capacity, dtype=jnp.int32) < live_count).astype(jnp.float32)  3.16 us
    gather x5, local copies, waits for them, and re-layouts, pick_blocks(): return jnp.take(blocks, slot_cols, axis=1)  3.01 us
    reshape x5, local copies, waits for them, and re-layouts, pick_blocks(): blocks = group_x.reshape(channels, -1, block_size)  2.54 us
    ppermute x1, starting transfers between devices, hold_the_field(): lax.ppermute(e_next, mesh_ax, rows)  2.07 us
  transfers between devices with their start and end apart: 5, of which 2 were waited for; matrix products, arithmetic and copies ran while one was open for 33% of the time, Pallas kernels for 0%

profile of v1, /device:TPU:1, one launch (start us, length us, event | category | flops | bytes accessed | tf_op | source)
XLA Modules:
  0.0 57.7 jit_solution(1596278789225275395)
XLA Ops:
  0.0 2.1 %collective-permute-start = (bf16[32,4096]{1,0:T(8,128)(2,1)}, bf16[32,4096]{1,0:T(8,128)(2,1)S(1)}, u32[]{:S(2)}, u32[]{:S(2)}) collective-permute-start(bf16[32,4096]{1,0:T(8,128)(2,1)} %param.7), channel_id=1, source_target_pairs={{0,1},{1,0},{2,3},{3,2},{4,5},{5,4},{6,7},{7,6},{8,9},{9,8},{10,11... | collective-permute-start | bytes 786440 | tf_op jit(solution)/shard_map/ppermute | solution.py:15
  2.1 1.0 %multiply_bitcast_fusion = f32[4,8,32,128]{3,1,2,0:T(8,128)S(1)} fusion(bf16[32,4096]{1,0:T(8,128)(2,1)} %param.7), kind=kLoop, calls=%fused_computation.58 | loop fusion | flops 262144 | bytes 786432
  3.1 0.7 %compare_and_fusion = (pred[32]{0:T(512)(128)(4,1)S(1)}, s32[32]{0:T(128)S(1)}, pred[32]{0:T(512)(128)(4,1)S(1)}, s32[32]{0:T(128)S(1)}, pred[32]{0:T(512)(128)(...) fusion(s32[1,1,5,32]{3,1,2,0:T(1,128)} %param.10), kind=kLoop, calls=%fused_computation.149 | loop fusion | flops 960 | bytes 1440 | tf_op jit(solution)/shard_map/jit(_take)/and | solution.py:44
  3.8 1.5 %fusion.113 = (s32[1,1,1]{2,1,0:T(1,128)}, s32[1,1,1]{2,1,0:T(1,128)}, s32[1,1,1]{2,1,0:T(1,128)}, s32[1,1,1]{2,1,0:T(1,128)}, s32[1,1,1]{2,1,0:T(1,128)}) fusion(s32[1,1,5]{2,1,0:T(1,128)} %param.11), kind=kLoop, calls=%fused_computation.174 | loop fusion | bytes 40 | tf_op jit(solution)/shard_map/slice | solution.py:69
  5.3 0.6 compare_convert_fusion.2
  5.9 0.7 %compare_convert_fusion.3 = f32[32]{0:T(128)S(1)} fusion(s32[]{:T(128)} %bitcast.21), kind=kLoop, calls=%fused_computation.157 | loop fusion | flops 64 | bytes 132 | tf_op jit(solution)/shard_map/convert_element_type | solution.py:33
  6.6 0.6 %compare_convert_fusion.1 = f32[32]{0:T(128)S(1)} fusion(s32[]{:T(128)} %bitcast.45), kind=kLoop, calls=%fused_computation.155 | loop fusion | flops 64 | bytes 132 | tf_op jit(solution)/shard_map/convert_element_type | solution.py:33
  7.3 0.6 %compare_convert_fusion.4 = f32[32]{0:T(128)S(1)} fusion(s32[]{:T(128)} %bitcast.9), kind=kLoop, calls=%fused_computation.158 | loop fusion | flops 64 | bytes 132 | tf_op jit(solution)/shard_map/convert_element_type | solution.py:33
  7.9 0.7 %compare_convert_fusion = f32[32]{0:T(128)S(1)} fusion(s32[]{:T(128)} %bitcast.57), kind=kLoop, calls=%fused_computation.154 | loop fusion | flops 64 | bytes 132 | tf_op jit(solution)/shard_map/convert_element_type | solution.py:33
  8.6 0.1 copy.76
  8.7 0.7 %slice_bitcast_fusion.10 = (s32[32]{0:T(128)S(1)}, s32[32]{0:T(128)S(1)}, s32[32]{0:T(128)S(1)}, s32[32]{0:T(128)S(1)}, s32[32]{0:T(128)S(1)}) fusion(s32[1,1,5,32]{3,1,2,0:T(1,128)} %param.9), kind=kLoop, calls=%fused_computation.159 | loop fusion | bytes 1280 | tf_op jit(solution)/shard_map/eq | solution.py:34
  9.4 0.0 collective-permute-done
  9.5 1.5 %fusion.37 = bf16[32,8192]{1,0:T(8,128)(2,1)S(1)} fusion(s32[]{:T(128)S(6)} %select_n.21, bf16[32,4096]{1,0:T(8,128)(2,1)} %param.7, bf16[32,4096]{1,0:T(8,128)(2,1)S(1)} %collective-permute-done), kind=kLoop, calls=%fused_computation.41 | loop fusion | flops 2097152 | bytes 1048580 | tf_op jit(solution)/shard_map/jit(_roll_dynamic)/concatenate | solution.py:17
  11.0 2.1 %collective-permute-start.1 = (bf16[32,8192]{1,0:T(8,128)(2,1)S(1)}, bf16[32,8192]{1,0:T(8,128)(2,1)S(1)}, u32[]{:S(2)}, u32[]{:S(2)}) collective-permute-start(bf16[32,8192]{1,0:T(8,128)(2,1)S(1)} %fusion.37), channel_id=1, source_target_pairs={{0,2},{2,4},{4,6},{6,8},{8,10},{10,12},{12,14},{14,16},{16,18},{18... | collective-permute-start | bytes 1572872 | tf_op jit(solution)/shard_map/ppermute | solution.py:22
  13.1 0.1 copy_bitcast_fusion.5
  13.2 0.1 collective-permute-start.3
  13.2 0.6 %gather_fusion = bf16[32,32,128]{2,1,0:T(8,128)(2,1)S(1)} fusion(bf16[32,64,128]{2,0,1:T(8,128)(2,1)S(1)} %copy_bitcast_fusion.5, s32[1024]{0:T(1024)S(1)} %pad_clamp_fusion.4), kind=kCustom, calls=%fused_computation.clone | custom fusion | bytes 524416 | tf_op jit(solution)/shard_map/jit(_take)/gather | solution.py:44
  13.8 2.4 %fusion.15 = f32[32,2,32,128]{3,2,1,0:T(8,128)S(1)} fusion(bf16[1,1,5,32,2,128,128]{6,5,4,3,2,1,0:T(8,128)(2,1)} %param.8, bf16[32,32,128]{2,1,0:T(8,128)(2,1)S(1)} %gather_fusion, pred[32]{0:T(512)(128)(4,1)S(1)} %get-tuple-element.25), kind=kOutput, calls=%fused_computation.20 | convolution fusion | flops 67239936 | bytes 3407904 | tf_op jit(solution)/shard_map/kprj,hkj->kphr/dot_general | solution.py:29
  16.4 0.1 pad_maximum_fusion
  16.4 8.4 %collective-permute-done.1 = bf16[32,8192]{1,0:T(8,128)(2,1)S(1)} collective-permute-done((bf16[32,8192]{1,0:T(8,128)(2,1)S(1)}, bf16[32,8192]{1,0:T(8,128)(2,1)S(1)}, u32[]{:S(2)}, u32[]{:S(2)}) %collective-permute-start.1) | collective-permute-done | bytes 524320 | tf_op jit(solution)/shard_map/ppermute | solution.py:22
  24.8 0.1 copy_bitcast_fusion.4
  24.9 0.6 %gather_fusion.1 = bf16[32,32,128]{2,1,0:T(8,128)(2,1)S(1)} fusion(bf16[32,64,128]{2,0,1:T(8,128)(2,1)S(1)} %copy_bitcast_fusion.4, s32[1024]{0:T(1024)S(1)} %pad_clamp_fusion.3), kind=kCustom, calls=%fused_computation.1.clone | custom fusion | bytes 524416 | tf_op jit(solution)/shard_map/jit(_take)/gather | solution.py:44
  25.5 2.4 %fusion.18 = f32[32,2,32,128]{3,2,1,0:T(8,128)S(1)} fusion(bf16[1,1,5,32,2,128,128]{6,5,4,3,2,1,0:T(8,128)(2,1)} %param.8, bf16[32,32,128]{2,1,0:T(8,128)(2,1)S(1)} %gather_fusion.1, pred[32]{0:T(512)(128)(4,1)S(1)} %get-tuple-element.23), kind=kOutput, calls=%fused_computation.21 | convolution fusion | flops 67239936 | bytes 3407904 | tf_op jit(solution)/shard_map/kprj,hkj->kphr/dot_general | solution.py:29
  28.0 0.0 collective-permute-done.3
  28.0 1.1 %copy_bitcast_fusion.2 = bf16[32,64,128]{2,0,1:T(8,128)(2,1)S(1)} fusion(bf16[32,8192]{1,0:T(8,128)(2,1)} %collective-permute-done.3), kind=kLoop, calls=%fused_computation.44 | loop fusion | bytes 1048576 | tf_op jit(solution)/shard_map/reshape | solution.py:43
  29.2 0.6 %gather_fusion.3 = bf16[32,32,128]{2,1,0:T(8,128)(2,1)S(1)} fusion(bf16[32,64,128]{2,0,1:T(8,128)(2,1)S(1)} %copy_bitcast_fusion.2, s32[1024]{0:T(1024)S(1)} %pad_clamp_fusion.1), kind=kCustom, calls=%fused_computation.3.clone | custom fusion | bytes 524416 | tf_op jit(solution)/shard_map/jit(_take)/gather | solution.py:44
  29.8 2.4 %fusion.24 = f32[32,2,32,128]{3,2,1,0:T(8,128)S(1)} fusion(bf16[1,1,5,32,2,128,128]{6,5,4,3,2,1,0:T(8,128)(2,1)} %param.8, bf16[32,32,128]{2,1,0:T(8,128)(2,1)S(1)} %gather_fusion.3, pred[32]{0:T(512)(128)(4,1)S(1)} %get-tuple-element.27), kind=kOutput, calls=%fused_computation.23 | convolution fusion | flops 67239936 | bytes 3407904 | tf_op jit(solution)/shard_map/kprj,hkj->kphr/dot_general | solution.py:29
  32.3 0.1 pad_maximum_fusion.1
  32.4 2.5 %collective-permute-start.2 = (bf16[32,8192]{1,0:T(8,128)(2,1)S(1)}, bf16[32,8192]{1,0:T(8,128)(2,1)S(1)}, u32[]{:S(2)}, u32[]{:S(2)}) collective-permute-start(bf16[32,8192]{1,0:T(8,128)(2,1)S(1)} %collective-permute-done.1), channel_id=1, source_target_pairs={{0,2},{2,4},{4,6},{6,8},{8,10},{10,12},{12,14},{14,16},{16,18},{18... | collective-permute-start | bytes 1572872 | tf_op jit(solution)/shard_map/ppermute | solution.py:22
  34.9 0.1 pad_maximum_fusion.3
  35.0 0.1 collective-permute-start.4
  35.0 0.9 %convolution_bitcast_fusion.3 = f32[32,32,128]{2,1,0:T(8,128)S(1)} fusion(f32[32,32,128]{2,1,0:T(8,128)S(1)} %pad_maximum_fusion.1, f32[32]{0:T(128)S(1)} %compare_convert_fusion.3, s32[32]{0:T(128)S(1)} %get-tuple-element.18), kind=kOutput, calls=%fused_computation.28 | convolution fusion | flops 50333696 | bytes 1048832 | tf_op jit(solution)/shard_map/kn,khr->hnr/dot_general | solution.py:38
  35.9 0.9 %convolution_bitcast_fusion.1 = f32[32,32,128]{2,1,0:T(8,128)S(1)} fusion(f32[32,32,128]{2,1,0:T(8,128)S(1)} %pad_maximum_fusion.3, f32[32]{0:T(128)S(1)} %compare_convert_fusion.1, s32[32]{0:T(128)S(1)} %get-tuple-element.20), kind=kOutput, calls=%fused_computation.26 | convolution fusion | flops 50333696 | bytes 1048832 | tf_op jit(solution)/shard_map/kn,khr->hnr/dot_general | solution.py:38
  36.9 9.3 %collective-permute-done.2 = bf16[32,8192]{1,0:T(8,128)(2,1)S(1)} collective-permute-done((bf16[32,8192]{1,0:T(8,128)(2,1)S(1)}, bf16[32,8192]{1,0:T(8,128)(2,1)S(1)}, u32[]{:S(2)}, u32[]{:S(2)}) %collective-permute-start.2) | collective-permute-done | bytes 524320 | tf_op jit(solution)/shard_map/ppermute | solution.py:22
  46.2 0.1 copy_bitcast_fusion.3
  46.3 0.6 %gather_fusion.2 = bf16[32,32,128]{2,1,0:T(8,128)(2,1)S(1)} fusion(bf16[32,64,128]{2,0,1:T(8,128)(2,1)S(1)} %copy_bitcast_fusion.3, s32[1024]{0:T(1024)S(1)} %pad_clamp_fusion.2), kind=kCustom, calls=%fused_computation.2.clone | custom fusion | bytes 524416 | tf_op jit(solution)/shard_map/jit(_take)/gather | solution.py:44
  46.9 2.4 %fusion.21 = f32[32,2,32,128]{3,2,1,0:T(8,128)S(1)} fusion(bf16[1,1,5,32,2,128,128]{6,5,4,3,2,1,0:T(8,128)(2,1)} %param.8, bf16[32,32,128]{2,1,0:T(8,128)(2,1)S(1)} %gather_fusion.2, pred[32]{0:T(512)(128)(4,1)S(1)} %get-tuple-element.21), kind=kOutput, calls=%fused_computation.22 | convolution fusion | flops 67239936 | bytes 3407904 | tf_op jit(solution)/shard_map/kprj,hkj->kphr/dot_general | solution.py:29
  49.4 0.0 collective-permute-done.4
  49.4 1.1 %copy_bitcast_fusion.1 = bf16[32,64,128]{2,0,1:T(8,128)(2,1)S(1)} fusion(bf16[32,8192]{1,0:T(8,128)(2,1)} %collective-permute-done.4), kind=kLoop, calls=%fused_computation.43 | loop fusion | bytes 1048576 | tf_op jit(solution)/shard_map/reshape | solution.py:43
  50.6 0.6 %gather_fusion.4 = bf16[32,32,128]{2,1,0:T(8,128)(2,1)S(1)} fusion(bf16[32,64,128]{2,0,1:T(8,128)(2,1)S(1)} %copy_bitcast_fusion.1, s32[1024]{0:T(1024)S(1)} %pad_clamp_fusion), kind=kCustom, calls=%fused_computation.4.clone | custom fusion | bytes 524416 | tf_op jit(solution)/shard_map/jit(_take)/gather | solution.py:44
  51.2 2.4 %fusion.27 = f32[32,2,32,128]{3,2,1,0:T(8,128)S(1)} fusion(bf16[1,1,5,32,2,128,128]{6,5,4,3,2,1,0:T(8,128)(2,1)} %param.8, bf16[32,32,128]{2,1,0:T(8,128)(2,1)S(1)} %gather_fusion.4, pred[32]{0:T(512)(128)(4,1)S(1)} %get-tuple-element.6), kind=kOutput, calls=%fused_computation.24 | convolution fusion | flops 67239936 | bytes 3407904 | tf_op jit(solution)/shard_map/kprj,hkj->kphr/dot_general | solution.py:29
  53.7 0.1 pad_maximum_fusion.2
  53.7 0.1 pad_maximum_fusion.4
  53.8 0.9 %convolution_bitcast_fusion.2 = f32[32,32,128]{2,1,0:T(8,128)S(1)} fusion(f32[32,32,128]{2,1,0:T(8,128)S(1)} %pad_maximum_fusion.2, f32[32]{0:T(128)S(1)} %compare_convert_fusion.2, s32[32]{0:T(128)S(1)} %get-tuple-element.17), kind=kOutput, calls=%fused_computation.27 | convolution fusion | flops 50333696 | bytes 1048832 | tf_op jit(solution)/shard_map/kn,khr->hnr/dot_general | solution.py:38
  54.7 1.0 %fusion.33 = f32[32,32,128]{2,1,0:T(8,128)S(1)} fusion(f32[32,32,128]{2,1,0:T(8,128)S(1)} %convolution_bitcast_fusion.1, f32[32,32,128]{2,1,0:T(8,128)S(1)} %convolution_bitcast_fusion.2, f32[32,32,128]{2,1,0:T(8,128)S(1)} %convolution_bitcast_fusion.3, f32[32,32,128]{2,1,0:T(8,128)S(1)} %bitcast.237, f32[32,32,128]{2,1,0:T(8,128)S(1)} %pad_maximum_fusion, ...), kind=kOutput, calls=%fused_computation.33 | convolution fusion | flops 50857984 | bytes 3145984 | tf_op jit(solution)/shard_map/kn,khr->hnr/dot_general | solution.py:38
  55.7 0.9 %fusion.34 = f32[32,32,128]{2,1,0:T(8,128)S(1)} fusion(f32[32,32,128]{2,1,0:T(8,128)S(1)} %fusion.33, f32[32,32,128]{2,1,0:T(8,128)S(1)} %pad_maximum_fusion.4, f32[32]{0:T(128)S(1)} %compare_convert_fusion, s32[32]{0:T(128)S(1)} %get-tuple-element.16), kind=kOutput, calls=%fused_computation.34 | convolution fusion | flops 50464768 | bytes 1573120 | tf_op jit(solution)/shard_map/kn,khr->hnr/dot_general | solution.py:38
  56.6 1.1 %copy.94 = f32[4,8,32,128]{3,1,2,0:T(8,128)} copy(f32[4,8,32,128]{3,2,1,0:T(8,128)S(1)} %bitcast.238) | data formatting | bytes 1048576
  (15 shorter events, 0.4 us)
Async XLA Ops:
  0.0 9.4 %collective-permute-start = (bf16[32,4096]{1,0:T(8,128)(2,1)}, bf16[32,4096]{1,0:T(8,128)(2,1)S(1)}, u32[]{:S(2)}, u32[]{:S(2)}) collective-permute-start(bf16[32,4096]{1,0:T(8,128)(2,1)} %param.7), channel_id=1, source_target_pairs={{0,1},{1,0},{2,3},{3,2},{4,5},{5,4},{6,7},{7,6},{8,9},{9,8},{10,11... | collective-permute-start | bytes 786440 | tf_op jit(solution)/shard_map/ppermute | solution.py:15
  11.0 13.8 %collective-permute-start.1 = (bf16[32,8192]{1,0:T(8,128)(2,1)S(1)}, bf16[32,8192]{1,0:T(8,128)(2,1)S(1)}, u32[]{:S(2)}, u32[]{:S(2)}) collective-permute-start(bf16[32,8192]{1,0:T(8,128)(2,1)S(1)} %fusion.37), channel_id=1, source_target_pairs={{0,2},{2,4},{4,6},{6,8},{8,10},{10,12},{12,14},{14,16},{16,18},{18... | collective-permute-start | bytes 1572872 | tf_op jit(solution)/shard_map/ppermute | solution.py:22
  13.2 14.9 %collective-permute-start.3 = (bf16[32,8192]{1,0:T(8,128)(2,1)S(1)}, bf16[32,8192]{1,0:T(8,128)(2,1)}, u32[]{:S(2)}, u32[]{:S(2)}) collective-permute-start(bf16[32,8192]{1,0:T(8,128)(2,1)S(1)} %fusion.37), channel_id=1, source_target_pairs={{0,30},{2,0},{4,2},{6,4},{8,6},{10,8},{12,10},{14,12},{16,14},{18,... | collective-permute-start | bytes 1572872 | tf_op jit(solution)/shard_map/ppermute | solution.py:22
  32.4 13.8 %collective-permute-start.2 = (bf16[32,8192]{1,0:T(8,128)(2,1)S(1)}, bf16[32,8192]{1,0:T(8,128)(2,1)S(1)}, u32[]{:S(2)}, u32[]{:S(2)}) collective-permute-start(bf16[32,8192]{1,0:T(8,128)(2,1)S(1)} %collective-permute-done.1), channel_id=1, source_target_pairs={{0,2},{2,4},{4,6},{6,8},{8,10},{10,12},{12,14},{14,16},{16,18},{18... | collective-permute-start | bytes 1572872 | tf_op jit(solution)/shard_map/ppermute | solution.py:22
  35.0 14.5 %collective-permute-start.4 = (bf16[32,8192]{1,0:T(8,128)(2,1)}, bf16[32,8192]{1,0:T(8,128)(2,1)}, u32[]{:S(2)}, u32[]{:S(2)}) collective-permute-start(bf16[32,8192]{1,0:T(8,128)(2,1)} %collective-permute-done.3), channel_id=1, source_target_pairs={{0,30},{2,0},{4,2},{6,4},{8,6},{10,8},{12,10},{14,12},{16,14},{18,... | collective-permute-start | bytes 1572872 | tf_op jit(solution)/shard_map/ppermute | solution.py:22
